TPU v7x, 512 devices: a whole 4x4x16 slice. The times are simulated.
512 devices in a mesh: pair: 64 (over z, x), int: 8 (over y, core).
Axes of the slice: x: 4, y: 4, z: 16, core: 2. Of those that a mesh axis runs over, the one named last changes fastest.
Arguments:
- amps: bfloat16 [512, 64, 4096], P('pair', None, 'int'), may hold values from -6 to 6
- amp_mask: int32 [512, 64], P('pair'), may hold values 0 or 1
- integrals: bfloat16 [64, 4096, 4096], P('pair', None, 'int'), may hold values from -0.09375 to 0.09375
- block_mask: int32 [64], P('pair'), may hold values 0 or 1
- in_tiles: int32 [64], replicated, may hold values from 0 to 63, each once
- out_tiles: int32 [64], replicated, may hold values from 0 to 63, each once
- vir_energy: float32 [1024], replicated, may hold values from 0.5 to 3
- pair_energy: float32 [512], P('pair'), may hold values from -4 to -1
- dressing: bfloat16 [1024, 1024], P('pair'), may hold values from -0.1875 to 0.1875
Outputs:
- new_amps: bfloat16 [512, 64, 4096], P('pair', None, 'int')
Inputs may be any that keep to these rules, and one draw needn't show every extreme that they name: `in_tiles`: a permutation of the 64 tiles. `out_tiles`: a permutation of the 64 tiles.
All inputs are finite; a program needn't handle non-finite values. No bound on the sum of `amp_mask` or of `block_mask` on one device may be relied on, other than what follows from the above.
Results may differ from a plain program's by a relative error of at most 0.0038.
Values may be sent and summed in bfloat16 or wider, within the bound.
A program may use at most 64 MiB of HBM per device.

v0:
```python
import jax
import jax.numpy as jnp
from jax import lax
from jax.sharding import PartitionSpec as P

TILE = 64
VT = 16
WA = 4


def shards(
    amps, amp_mask, integrals, block_mask, in_tiles, out_tiles, vir_energy, pair_energy, dressing
):
    local_pairs, tile_count, share_size = amps.shape
    strip_rows = share_size // TILE
    int_index = lax.axis_index("int")
    masked = jnp.where(amp_mask[:, :, None] > 0, amps, jnp.zeros_like(amps))
    ordered = jnp.take(masked, in_tiles, axis=1)
    received = lax.all_to_all(ordered, "pair", split_axis=1, concat_axis=0, tiled=True)
    partial_value = jnp.einsum(
        "psk,sak->psa", received, integrals, preferred_element_type=jnp.float32
    )
    partial_value = partial_value * block_mask.astype(jnp.float32)[None, :, None]
    partial_value = lax.optimization_barrier(partial_value.astype(jnp.bfloat16)).astype(jnp.float32)
    summed = lax.psum(partial_value.astype(jnp.bfloat16), "int").astype(jnp.float32)
    own_share = lax.dynamic_slice_in_dim(summed, int_index * share_size, share_size, 2)
    returned = lax.all_to_all(
        own_share.astype(jnp.bfloat16), "pair", split_axis=0, concat_axis=1, tiled=True
    ).astype(own_share.dtype)
    slot_of = (
        jnp.zeros((tile_count,), jnp.int32)
        .at[out_tiles]
        .set(jnp.arange(tile_count, dtype=jnp.int32))
    )
    ladder_terms = jnp.take(returned, slot_of, axis=1)
    tile_rows = masked.reshape(local_pairs, WA, VT, strip_rows, TILE)
    tile_rows = jnp.transpose(tile_rows, (0, 1, 3, 2, 4)).reshape(
        local_pairs * WA * strip_rows, VT * TILE
    )
    running = jnp.dot(
        tile_rows,
        lax.all_gather(dressing, "pair", axis=0, tiled=True),
        preferred_element_type=jnp.float32,
    )
    running = running.reshape(local_pairs, WA, strip_rows, VT, TILE)
    cycle_terms = jnp.transpose(running, (0, 1, 3, 2, 4)).reshape(
        local_pairs, tile_count, share_size
    )
    energies = vir_energy.reshape(VT, TILE)
    own_energy = lax.dynamic_slice_in_dim(energies[:WA], int_index * strip_rows, strip_rows, 1)
    denominator = (
        pair_energy[:, None, None, None, None]
        - own_energy[None, :, None, :, None]
        - energies[None, None, :, None, :]
    )
    denominator = denominator.reshape(local_pairs, tile_count, share_size)
    updated = masked.astype(jnp.float32) + (ladder_terms + cycle_terms) / denominator
    return updated.astype(jnp.bfloat16)


def solution(mesh):
    in_specs = (
        P("pair", None, "int"),
        P("pair", None),
        P("pair", None, "int"),
        P("pair"),
        P(),
        P(),
        P(),
        P("pair"),
        P("pair", None),
    )
    out_specs = P("pair", None, "int")
    return jax.shard_map(shards, mesh=mesh, in_specs=in_specs, out_specs=out_specs, check_vma=False)
```

profile of v0, /device:TPU:16, one launch (start us, length us, event | category | flops | bytes accessed | tf_op | source)
XLA Modules:
  0.0 241.5 jit_solution(16358082051121928171)
XLA Ops:
  7.4 0.7 broadcast_compare_fusion
  8.2 0.7 compare_and_fusion
  8.8 0.7 compare_select_fusion
  9.5 1.4 copy_select_fusion
  10.9 0.6 gather_fusion
  11.5 0.9 select_bitcast_fusion
  12.4 18.6 %all-to-all-start = ((bf16[8,64,512]{2,0,1:T(8,128)(2,1)}), bf16[8,64,512]{2,0,1:T(8,128)(2,1)S(1)}, u32[]{:S(2)}, u32[]{:S(2)}) async-start(bf16[8,64,512]{2,0,1:T(8,128)(2,1)} %select_bitcast_fusion), calls=%async_computation | async-start | bytes 1048576 | tf_op jit(solution)/shard_map/all_to_all | solution.py:19
  31.7 32.1 %all-to-all-done = bf16[8,64,512]{2,0,1:T(8,128)(2,1)S(1)} async-done(((bf16[8,64,512]{2,0,1:T(8,128)(2,1)}), bf16[8,64,512]{2,0,1:T(8,128)(2,1)S(1)}, u32[]{:S(2)}, u32[]{:S(2)}) %all-to-all-start) | async-done | bytes 524320 | tf_op jit(solution)/shard_map/all_to_all | solution.py:19
  63.8 6.5 %fusion = bf16[512,1,4096]{2,0,1:T(8,128)(2,1)} fusion(bf16[1,4096,512]{2,1,0:T(8,128)(2,1)} %param.11, f32[]{:T(128)} %bitcast.5, bf16[8,64,512]{2,0,1:T(8,128)(2,1)S(1)} %all-to-all-done), kind=kOutput, calls=%fused_computation.4 | convolution fusion | flops 2151677952 | bytes 8912900 | tf_op jit(solution)/shard_map/psk,sak->psa/dot_general | solution.py:20
  70.4 0.5 all-gather.2.cloned.1.call-update
  70.9 75.6 %all-reduce.2.cloned.1.call-done = bf16[512,1,4096]{2,0,1:T(8,128)(2,1)} async-done(((bf16[512,1,4096]{2,0,1:T(8,128)(2,1)}), bf16[512,1,4096]{2,0,1:T(8,128)(2,1)}) %all-reduce.2.cloned.1.call-update) | async-done | bytes 4194320 | tf_op jit(solution)/shard_map/psum | solution.py:25
  146.6 1.1 convert_convert_fusion
  147.7 0.5 broadcast.65
  148.2 1.0 reduce
  149.2 1.0 reshape.101
  150.2 15.8 %all-to-all-start.1 = ((bf16[64,2,2048]{2,1,0:T(2,128)(2,1)}), bf16[64,2,2048]{2,1,0:T(2,128)(2,1)}, u32[]{:S(2)}, u32[]{:S(2)}) async-start(bf16[64,2,2048]{2,1,0:T(2,128)(2,1)} %reshape.101), calls=%async_computation.1 | async-start | bytes 1048576 | tf_op jit(solution)/shard_map/all_to_all | solution.py:27
  166.0 1.5 reshape.65
  167.8 0.3 sub.43
  168.1 0.5 sub.44
  168.6 2.4 %copy.21 = bf16[8,4,8,16,64]{4,3,2,1,0:T(8,128)(2,1)S(1)} copy(bf16[8,4,8,16,64]{4,2,0,3,1:T(8,128)(2,1)} %bitcast.60) | data formatting | bytes 1048576 | tf_op jit(solution)/shard_map/transpose | solution.py:37
  171.1 1.5 reshape.96
  172.6 0.1 sub.47
  172.7 1.0 scatter_custom_fusion
  173.7 42.3 %all-gather.2.cloned.1.call-done = bf16[1024,1024]{1,0:T(8,128)(2,1)} async-done(((bf16[16,1024]{1,0:T(8,128)(2,1)}), bf16[1024,1024]{1,0:T(8,128)(2,1)}) %all-gather.2.cloned.1.call-update) | async-done | bytes 2097168 | tf_op jit(solution)/shard_map/all_gather | solution.py:42
  216.0 2.9 %copy.22 = bf16[1024,1024]{1,0:T(8,128)(2,1)S(1)} copy(bf16[1024,1024]{0,1:T(8,128)(2,1)} %bitcast.61) | data formatting | bytes 4194304 | tf_op jit(solution)/shard_map/dot_general | solution.py:40
  218.9 3.7 %convolution_bitcast_fusion = f32[8,4,16,8,64]{4,3,2,1,0:T(8,128)} fusion(bf16[16,64,1024,1,1]{2,1,0,4,3:T(8,128)(2,1)S(1)} %bitcast.62, bf16[8,4,8,1024,1]{3,2,1,0,4:T(8,128)(2,1)} %reshape.96), kind=kOutput, calls=%fused_computation.6 | convolution fusion | flops 536870912 | bytes 3670016 | tf_op jit(solution)/shard_map/dot_general | solution.py:40
  222.6 1.9 reshape.66
  224.5 3.6 %reshape.102 = bf16[512,1,512]{2,1,0:T(2,128)(2,1)S(1)} reshape(bf16[64,2,2048]{2,1,0:T(2,128)(2,1)} %all-to-all-done.1) | data formatting | bytes 1048576
  228.1 1.1 copy.33
  229.2 1.8 gather_fusion.1
  231.1 2.1 fusion.4
  233.1 0.9 copy.24
  (21 shorter events, 0.6 us)
Async XLA Ops:
  12.4 51.4 %all-to-all-start = ((bf16[8,64,512]{2,0,1:T(8,128)(2,1)}), bf16[8,64,512]{2,0,1:T(8,128)(2,1)S(1)}, u32[]{:S(2)}, u32[]{:S(2)}) async-start(bf16[8,64,512]{2,0,1:T(8,128)(2,1)} %select_bitcast_fusion), calls=%async_computation | async-start | bytes 1048576 | tf_op jit(solution)/shard_map/all_to_all | solution.py:19
  31.0 115.6 %all-reduce.2.cloned.1.call-start = ((), (), s32[]{:S(2)}) async-start(), calls=%async_computation.2 | async-start | bytes 8388608 | tf_op jit(solution)/shard_map/psum | solution.py:25
  70.3 97.2 %copy-start = (f32[1024]{0:T(1024)S(1)}, f32[1024]{0:T(1024)}, u32[]{:S(2)}) copy-start(f32[1024]{0:T(1024)} %param.15) | copy-start | bytes 12292
  70.3 97.3 %slice-start = ((f32[1024]{0:T(1024)}), f32[256]{0:T(256)S(1)}, s32[]{:S(2)}) async-start(f32[1024]{0:T(1024)} %param.15), calls=%async_computation.4 | async-start | bytes 2048 | tf_op jit(solution)/shard_map/slice | solution.py:50
  70.3 97.4 %copy-start.1 = (f32[8]{0:T(128)S(1)}, f32[8]{0:T(128)}, u32[]{:S(2)}) copy-start(f32[8]{0:T(128)} %param.16) | copy-start | bytes 100
  70.4 145.7 %all-gather.2.cloned.1.call-start = ((), (), s32[]{:S(2)}) async-start(), calls=%async_computation.3 | async-start | bytes 2129920 | tf_op jit(solution)/shard_map/all_gather | solution.py:42
  150.2 74.3 %all-to-all-start.1 = ((bf16[64,2,2048]{2,1,0:T(2,128)(2,1)}), bf16[64,2,2048]{2,1,0:T(2,128)(2,1)}, u32[]{:S(2)}, u32[]{:S(2)}) async-start(bf16[64,2,2048]{2,1,0:T(2,128)(2,1)} %reshape.101), calls=%async_computation.1 | async-start | bytes 1048576 | tf_op jit(solution)/shard_map/all_to_all | solution.py:27
Sparse Core Ops, SparseCore 0:
  70.5 76.0 all-reduce.1
Sparse Core Ops, SparseCore 1:
  73.8 142.2 all-gather.1
where the time goes:
time: 242 us
  waiting for transfers between devices  151 us (62%)
  starting transfers between devices  34.4 us (14%)
  local copies, waits for them, and re-layouts  22.1 us (9%)
  between operations  15.6 us (6%)
  matrix products  10.2 us (4%)
  other arithmetic  8.61 us (4%)
    psum x1, waiting for transfers between devices, shards(): lax.psum(partial_value.astype(jnp.bfloat16), 'int').astype(jnp.float32)  75.6 us
    all_gather x1, waiting for transfers between devices, shards(): lax.all_gather(dressing, 'pair', axis=0, tiled=True)  42.3 us
    all_to_all x1, waiting for transfers between devices, shards(): lax.all_to_all(ordered, 'pair', split_axis=1, concat_axis=0, tiled=True)  32.1 us
    all_to_all x1, starting transfers between devices, shards(): lax.all_to_all(ordered, 'pair', split_axis=1, concat_axis=0, tiled=True)  18.6 us
    all_to_all x1, starting transfers between devices, shards(): lax.all_to_all(own_share.astype(jnp.bfloat16), 'pair', split_axis=0, conc...  15.8 us
    dot_general x1, matrix products, shards(): jnp.einsum('psk,sak->psa', received, integrals, preferred_element_type=jn...  6.51 us
    unnamed x7, local copies, waits for them, and re-layouts  5.7 us
  transfers between devices with their start and end apart: 4, of which 3 were waited for; matrix products, arithmetic and copies ran while one was open for 8% of the time, Pallas kernels for 0%

commit v1 on v0

--- a/solution.py
+++ b/solution.py
@@ -39,7 +39,9 @@
     )
     running = jnp.dot(
         tile_rows,
-        lax.all_gather(dressing, "pair", axis=0, tiled=True),
+        jnp.concatenate(
+            lax.all_to_all(jnp.stack([dressing] * lax.axis_size("pair")), "pair", 0, 0), axis=0
+        ),
         preferred_element_type=jnp.float32,
     )
     running = running.reshape(local_pairs, WA, strip_rows, VT, TILE)

time: 242 us -> 326 us (1.35)
  the two profiles are of different devices: /device:TPU:16 before, /device:TPU:24 now
where the time goes in v1:
time: 326 us; the launch traced here: 325 us
  waiting for transfers between devices  188 us (58%)
  blocking collectives  48.6 us (15%)
  local copies, waits for them, and re-layouts  30.5 us (9%)
  starting transfers between devices  24.8 us (8%)
  between operations  14.2 us (4%)
  matrix products  10.9 us (3%)
  other arithmetic  8.61 us (3%)
    all_to_all x1, waiting for transfers between devices, shards(): lax.all_to_all(jnp.stack([dressing] * lax.axis_size('pair')), 'pair', 0, 0)  78.8 us
    psum x1, waiting for transfers between devices, shards(): lax.psum(partial_value.astype(jnp.bfloat16), 'int').astype(jnp.float32)  76.8 us
    all_to_all x1, blocking collectives, shards(): lax.all_to_all(own_share.astype(jnp.bfloat16), 'pair', split_axis=0, conc...  48.6 us
    all_to_all x1, waiting for transfers between devices, shards(): lax.all_to_all(ordered, 'pair', split_axis=1, concat_axis=0, tiled=True)  32.1 us
    all_to_all x1, starting transfers between devices, shards(): lax.all_to_all(ordered, 'pair', split_axis=1, concat_axis=0, tiled=True)  18.6 us
    unnamed x11, local copies, waits for them, and re-layouts  6.98 us
  transfers between devices with their start and end apart: 3, of which 3 were waited for; matrix products, arithmetic and copies ran while one was open for 7% of the time, Pallas kernels for 0%

profile of v1, /device:TPU:24, one launch (start us, length us, event | category | flops | bytes accessed | tf_op | source)
XLA Modules:
  0.0 325.4 jit_solution(5936950947498881350)
XLA Ops:
  6.5 0.7 broadcast_compare_fusion
  7.3 0.7 compare_and_fusion
  8.0 0.7 compare_select_fusion
  8.7 1.4 copy_select_fusion
  10.1 0.6 gather_fusion
  10.7 0.9 select_bitcast_fusion
  11.6 18.6 %all-to-all-start = ((bf16[8,64,512]{2,0,1:T(8,128)(2,1)}), bf16[8,64,512]{2,0,1:T(8,128)(2,1)S(1)}, u32[]{:S(2)}, u32[]{:S(2)}) async-start(bf16[8,64,512]{2,0,1:T(8,128)(2,1)} %select_bitcast_fusion), calls=%async_computation | async-start | bytes 1048576 | tf_op jit(solution)/shard_map/all_to_all | solution.py:19
  30.9 32.1 %all-to-all-done = bf16[8,64,512]{2,0,1:T(8,128)(2,1)S(1)} async-done(((bf16[8,64,512]{2,0,1:T(8,128)(2,1)}), bf16[8,64,512]{2,0,1:T(8,128)(2,1)S(1)}, u32[]{:S(2)}, u32[]{:S(2)}) %all-to-all-start) | async-done | bytes 524320 | tf_op jit(solution)/shard_map/all_to_all | solution.py:19
  63.0 6.5 %fusion = bf16[512,1,4096]{2,0,1:T(8,128)(2,1)} fusion(bf16[1,4096,512]{2,1,0:T(8,128)(2,1)} %param.11, f32[]{:T(128)} %bitcast.5, bf16[8,64,512]{2,0,1:T(8,128)(2,1)S(1)} %all-to-all-done), kind=kOutput, calls=%fused_computation.4 | convolution fusion | flops 2151677952 | bytes 8912900 | tf_op jit(solution)/shard_map/psk,sak->psa/dot_general | solution.py:20
  69.5 76.8 %all-reduce.2.cloned.1.call-done = bf16[512,1,4096]{2,0,1:T(8,128)(2,1)} async-done(((bf16[512,1,4096]{2,0,1:T(8,128)(2,1)}), bf16[512,1,4096]{2,0,1:T(8,128)(2,1)}) %all-reduce.2.cloned.1.call-update) | async-done | bytes 4194320 | tf_op jit(solution)/shard_map/psum | solution.py:25
  146.4 1.1 convert_convert_fusion
  147.4 0.5 broadcast.67
  147.9 1.0 reduce
  149.0 0.2 reshape.107
  149.2 48.6 %all_to_all.29 = bf16[64,2,2048]{2,1,0:T(2,128)(2,1)} all-to-all(bf16[64,2,2048]{2,1,0:T(2,128)(2,1)S(1)} %reshape.107), channel_id=1, replica_groups=mesh['pair'=64,'int'=8] {'pair'}, dimensions={0} | all-to-all | bytes 1048576 | tf_op jit(solution)/shard_map/all_to_all | solution.py:27
  197.8 1.6 stack.2
  199.4 6.2 %all-to-all-start.2 = ((bf16[64,16,1024]{2,1,0:T(8,128)(2,1)}), bf16[64,16,1024]{2,1,0:T(8,128)(2,1)S(1)}, u32[]{:S(2)}, u32[]{:S(2)}) async-start(bf16[64,16,1024]{2,1,0:T(8,128)(2,1)} %stack.2), calls=%async_computation.2 | async-start | bytes 4194304 | tf_op jit(solution)/shard_map/all_to_all | solution.py:43
  205.7 1.5 reshape.70
  207.5 1.6 sub.43
  209.1 1.9 sub.44
  211.1 3.4 %copy.21 = bf16[8,4,8,16,64]{4,3,2,1,0:T(8,128)(2,1)} copy(bf16[8,4,8,16,64]{4,2,0,3,1:T(8,128)(2,1)} %bitcast.63) | data formatting | bytes 1048576 | tf_op jit(solution)/shard_map/transpose | solution.py:37
  214.5 2.6 reshape.102
  217.3 1.0 scatter_custom_fusion
  218.3 4.5 %reshape.108 = bf16[512,1,512]{2,1,0:T(2,128)(2,1)} reshape(bf16[64,2,2048]{2,1,0:T(2,128)(2,1)} %all_to_all.29) | data formatting | bytes 1048576
  222.7 2.3 copy.33
  225.0 2.8 gather_fusion.1
  227.8 78.8 %all-to-all-done.2 = bf16[64,16,1024]{2,1,0:T(8,128)(2,1)S(1)} async-done(((bf16[64,16,1024]{2,1,0:T(8,128)(2,1)}), bf16[64,16,1024]{2,1,0:T(8,128)(2,1)S(1)}, u32[]{:S(2)}, u32[]{:S(2)}) %all-to-all-start.2) | async-done | bytes 2097184 | tf_op jit(solution)/shard_map/all_to_all | solution.py:43
  306.6 2.6 copy.22
  309.2 4.4 %convolution_bitcast_fusion = f32[8,4,16,8,64]{4,3,2,1,0:T(8,128)} fusion(bf16[16,64,1024,1,1]{2,1,0,4,3:T(8,128)(2,1)} %bitcast.64, bf16[8,4,8,1024,1]{3,2,1,0,4:T(8,128)(2,1)} %reshape.102), kind=kOutput, calls=%fused_computation.6 | convolution fusion | flops 536870912 | bytes 3670016 | tf_op jit(solution)/shard_map/dot_general | solution.py:40
  313.6 1.9 reshape.72
  315.6 2.1 fusion.4
  317.6 0.9 copy.24
  (24 shorter events, 0.6 us)
Async XLA Ops:
  11.6 51.4 %all-to-all-start = ((bf16[8,64,512]{2,0,1:T(8,128)(2,1)}), bf16[8,64,512]{2,0,1:T(8,128)(2,1)S(1)}, u32[]{:S(2)}, u32[]{:S(2)}) async-start(bf16[8,64,512]{2,0,1:T(8,128)(2,1)} %select_bitcast_fusion), calls=%async_computation | async-start | bytes 1048576 | tf_op jit(solution)/shard_map/all_to_all | solution.py:19
  30.2 116.2 %all-reduce.2.cloned.1.call-start = ((), (), s32[]{:S(2)}) async-start(), calls=%async_computation.3 | async-start | bytes 8388608 | tf_op jit(solution)/shard_map/psum | solution.py:25
  69.5 128.3 %copy-start.1 = (bf16[16,1024]{1,0:T(8,128)(2,1)S(1)}, bf16[16,1024]{1,0:T(8,128)(2,1)}, u32[]{:S(2)}) copy-start(bf16[16,1024]{1,0:T(8,128)(2,1)} %param.17) | copy-start | bytes 98308
  197.8 9.4 %copy-start.2 = (f32[1024]{0:T(1024)S(1)}, f32[1024]{0:T(1024)}, u32[]{:S(2)}) copy-start(f32[1024]{0:T(1024)} %param.15) | copy-start | bytes 12292
  197.8 9.5 %slice-start = ((f32[1024]{0:T(1024)}), f32[256]{0:T(256)S(1)}, s32[]{:S(2)}) async-start(f32[1024]{0:T(1024)} %param.15), calls=%async_computation.4 | async-start | bytes 2048 | tf_op jit(solution)/shard_map/slice | solution.py:52
  197.8 9.6 %copy-start.3 = (f32[8]{0:T(128)S(1)}, f32[8]{0:T(128)}, u32[]{:S(2)}) copy-start(f32[8]{0:T(128)} %param.16) | copy-start | bytes 100
  199.4 107.2 %all-to-all-start.2 = ((bf16[64,16,1024]{2,1,0:T(8,128)(2,1)}), bf16[64,16,1024]{2,1,0:T(8,128)(2,1)S(1)}, u32[]{:S(2)}, u32[]{:S(2)}) async-start(bf16[64,16,1024]{2,1,0:T(8,128)(2,1)} %stack.2), calls=%async_computation.2 | async-start | bytes 4194304 | tf_op jit(solution)/shard_map/all_to_all | solution.py:43
  309.2 6.4 %copy-start = (f32[64,8,512]{2,1,0:T(8,128)S(1)}, f32[64,8,512]{2,1,0:T(8,128)}, u32[]{:S(2)}) copy-start(f32[64,8,512]{2,1,0:T(8,128)} %gather_fusion.1) | copy-start | bytes 3145732
Sparse Core Ops, SparseCore 0:
  69.6 76.6 all-reduce.1
